TPU v7x, 256 devices: a whole 4x4x8 slice. The times are simulated.
256 devices in a mesh: clip: 32 (over z_hi, x, y), tm: 8 (over z_lo, core).
Axes of the slice: x: 4, y: 4, z: 8 (z_hi: 2, z_lo: 4; z = z_hi * 4 + z_lo), core: 2. Of those that a mesh axis runs over, the one named last changes fastest.
Arguments:
- audio_feats: bfloat16 [128, 2048, 256], P('clip', 'tm'), may hold values from -6 to 6
- lip_feats: bfloat16 [128, 2048, 256], P('clip', 'tm'), may hold values from -6 to 6
- lengths: int32 [128], P('clip'), may hold values from 1024 to 2048
- labels: int32 [128], P('clip'), may hold values from -15 to 15
- w_audio_conv: bfloat16 [3, 256, 512], replicated, may hold values from -0.21875 to 0.21875
- w_audio_proj: bfloat16 [512, 512], replicated, may hold values from -0.25 to 0.25
- w_lip_conv: bfloat16 [3, 256, 512], replicated, may hold values from -0.21875 to 0.21875
- w_lip_proj: bfloat16 [512, 512], replicated, may hold values from -0.25 to 0.25
Outputs:
- loss: float32 [], replicated
- grad_audio_conv: float32 [3, 256, 512], replicated
- grad_audio_proj: float32 [512, 512], replicated
- grad_lip_conv: float32 [3, 256, 512], replicated
- grad_lip_proj: float32 [512, 512], replicated
All inputs are finite; a program needn't handle non-finite values.
Results may differ from a plain program's by a relative error of at most 0.0075.
Values may be sent and summed in bfloat16 or wider, within the bound.
A program may use at most 64 MiB of HBM per device.

v0:
```python
import jax
import jax.numpy as jnp
from jax import lax
from jax.sharding import PartitionSpec as P

SPAN = 15
logit_sharpening_divisor = 10.0
loss_scale = 1024.0
epsilon = 1e-06


def padded_2(cells, sides, width):
    for axis, dim in sides:
        count = lax.axis_size(axis)
        ends = count - 1
        head = lax.slice_in_dim(cells, 0, width, axis=dim)
        tail = lax.slice_in_dim(cells, cells.shape[dim] - width, cells.shape[dim], axis=dim)
        cells = jnp.concatenate(
            [
                lax.ppermute(tail, axis, [(i, (i + 1) % count) for i in range(ends)]),
                cells,
                lax.ppermute(head, axis, [((i + 1) % count, i) for i in range(ends)]),
            ],
            axis=dim,
        )
    return cells


def from_behind(value, axis, steps):
    count = lax.axis_size(axis)
    initial, last = (max(0, -steps), min(count, count - steps))
    return lax.ppermute(value, axis, [(source, source + steps) for source in range(initial, last)])


def silu_slope(values):
    sigma = jax.nn.sigmoid(values)
    return sigma * (1.0 + values * (1.0 - sigma))


def encoder(padded, w_conv, w_proj):
    clip_num, frame_pad, chan_num = padded.shape
    frame_num = frame_pad - 2
    columns = jnp.concatenate(
        [padded[:, 0:frame_num], padded[:, 1 : frame_num + 1], padded[:, 2 : frame_num + 2]], axis=2
    )
    before = jnp.einsum(
        "cfk,ke->cfe",
        columns,
        w_conv.reshape(3 * chan_num, w_conv.shape[2]),
        preferred_element_type=jnp.float32,
    )
    hidden = jax.nn.silu(before).astype(jnp.bfloat16)
    embedded = jnp.einsum("cfe,eg->cfg", hidden, w_proj, preferred_element_type=jnp.float32).astype(
        jnp.bfloat16
    )
    return (columns, before, hidden, embedded)


def inverse_norm(embedded):
    values = embedded.astype(jnp.float32)
    return lax.rsqrt(jnp.sum(values * values, axis=-1) + epsilon)


def spread_band(band, wide_len):
    clip_num, row_num, band_len = band.shape
    full_band = jnp.pad(band, ((0, 0), (0, 0), (0, wide_len + 1 - band_len)))
    flat_band = full_band.reshape(clip_num, row_num * (wide_len + 1))[:, : row_num * wide_len]
    return flat_band.reshape(clip_num, row_num, wide_len)


def narrow_band(matrix, band_len):
    clip_num, row_num, wide_len = matrix.shape
    flat_mat = jnp.pad(matrix.reshape(clip_num, row_num * wide_len), ((0, 0), (0, row_num)))
    return flat_mat.reshape(clip_num, row_num, wide_len + 1)[:, :, :band_len]


def flatten_rows(values):
    return values.reshape(values.shape[0] * values.shape[1], values.shape[2])


def proj_grad(hidden, grad_emb):
    return jnp.einsum("re,rf->ef", hidden, grad_emb, preferred_element_type=jnp.float32)


def conv_grad(columns, before, grad_emb, w_proj, w_conv):
    grad_hidden = jnp.einsum("rf,ef->re", grad_emb, w_proj, preferred_element_type=jnp.float32)
    grad_before = (grad_hidden * silu_slope(before)).astype(jnp.bfloat16)
    grad_conv = jnp.einsum("rk,re->ke", columns, grad_before, preferred_element_type=jnp.float32)
    return grad_conv.reshape(w_conv.shape)


def shards(
    audio_feats, lip_feats, lengths, labels, w_audio_conv, w_audio_proj, w_lip_conv, w_lip_proj
):
    clip_num, frame_num, chan_num = audio_feats.shape
    width = w_audio_proj.shape[1]
    offsets = 2 * SPAN + 1
    wide_len = frame_num + 2 * SPAN
    first_frame = lax.axis_index("tm") * frame_num
    stacked = jnp.stack([audio_feats, lip_feats])
    padded = padded_2(stacked, (("tm", 2),), 1)
    cols_a, pre_a, hid_a, emb_a = encoder(padded[0], w_audio_conv, w_audio_proj)
    cols_v, pre_v, hid_v, emb_v = encoder(padded[1], w_lip_conv, w_lip_proj)
    window = padded_2(emb_a, (("tm", 1),), SPAN)
    cols_a, pre_a, hid_a = (flatten_rows(cols_a), flatten_rows(pre_a), flatten_rows(hid_a))
    cols_v, pre_v, hid_v = (flatten_rows(cols_v), flatten_rows(pre_v), flatten_rows(hid_v))
    count = lax.psum(jnp.sum((lengths - jnp.abs(labels)).astype(jnp.float32)), "clip")
    matrix = jnp.einsum("cfe,cwe->cfw", emb_v, window, preferred_element_type=jnp.float32)
    lagged_inner_terms = narrow_band(matrix, offsets)
    inv_win = inverse_norm(window)
    reciprocal_visual_length = inverse_norm(emb_v)
    reciprocal_lag_strip = jnp.stack(
        [inv_win[:, offset : offset + frame_num] for offset in range(offsets)], axis=2
    )
    frame_ids = first_frame + jnp.arange(frame_num, dtype=jnp.int32)
    shifts = jnp.arange(offsets, dtype=jnp.int32) - SPAN
    positions = frame_ids[:, None] + shifts[None, :]
    inside = frame_ids[None, :] < lengths[:, None]
    valid = inside[:, :, None] & (positions[None] >= 0) & (positions[None] < lengths[:, None, None])
    target_pos = frame_ids[None, :] + labels[:, None]
    counted = inside & (target_pos >= 0) & (target_pos < lengths[:, None])
    correct_lag_position = (shifts[None, :] == labels[:, None]).astype(jnp.float32)
    lag_similarity_logits = (
        logit_sharpening_divisor
        * lagged_inner_terms
        * reciprocal_visual_length[:, :, None]
        * reciprocal_lag_strip
    )
    exponentiated_logits = jnp.where(valid, jnp.exp(lag_similarity_logits), 0.0)
    partition_sums = jnp.where(inside, jnp.sum(exponentiated_logits, axis=2), 1.0)
    picked = jnp.sum(lag_similarity_logits * correct_lag_position[:, None, :], axis=2)
    loss_local = jnp.sum(jnp.where(counted, jnp.log(partition_sums) - picked, 0.0))
    normalized_probabilities = jnp.where(counted, loss_scale / count, 0.0)
    logit_derivative = (
        logit_sharpening_divisor
        * normalized_probabilities[:, :, None]
        * (exponentiated_logits / partition_sums[:, :, None] - correct_lag_position[:, None, :])
    )
    grad_dots = (
        logit_derivative * reciprocal_visual_length[:, :, None] * reciprocal_lag_strip
    ).astype(jnp.bfloat16)
    grad_inv_v = jnp.sum(logit_derivative * lagged_inner_terms * reciprocal_lag_strip, axis=2)
    grad_inv_win = jnp.sum(
        spread_band(
            logit_derivative * lagged_inner_terms * reciprocal_visual_length[:, :, None], wide_len
        ),
        axis=1,
    )
    band_full = spread_band(grad_dots, wide_len)
    lip_sum = jnp.einsum("cfw,cwe->cfe", band_full, window, preferred_element_type=jnp.float32)
    lip_vals = emb_v.astype(jnp.float32)
    grad_lip = (
        lip_sum
        - (
            reciprocal_visual_length
            * reciprocal_visual_length
            * reciprocal_visual_length
            * grad_inv_v
        )[:, :, None]
        * lip_vals
    ).astype(jnp.bfloat16)
    win_sum = jnp.einsum("cfw,cfe->cwe", band_full, emb_v, preferred_element_type=jnp.float32)
    win_sum = win_sum - (inv_win * inv_win * inv_win * grad_inv_win)[:, :, None] * window.astype(
        jnp.float32
    )
    own_grad = win_sum[:, SPAN : SPAN + frame_num]
    from_after = from_behind(win_sum[:, :SPAN], "tm", -1)
    from_before = from_behind(win_sum[:, frame_num + SPAN :], "tm", 1)
    own_grad = own_grad.at[:, frame_num - SPAN :].add(from_after)
    own_grad = own_grad.at[:, :SPAN].add(from_before)
    grad_audio = own_grad.astype(jnp.bfloat16).reshape(clip_num * frame_num, width)
    grad_lip = grad_lip.reshape(clip_num * frame_num, width)
    grad_ap = proj_grad(hid_a, grad_audio)
    grad_vp = proj_grad(hid_v, grad_lip)
    grad_ac = conv_grad(cols_a, pre_a, grad_audio, w_audio_proj, w_audio_conv)
    grad_vc = conv_grad(cols_v, pre_v, grad_lip, w_lip_proj, w_lip_conv)
    grad_ac, grad_vc, grad_ap, grad_vp, loss_sum = lax.psum(
        (grad_ac, grad_vc, grad_ap, grad_vp, loss_local), ("clip", "tm")
    )
    return (loss_sum / count, grad_ac, grad_ap, grad_vc, grad_vp)


def solution(mesh):
    placed = (
        P("clip", "tm", None),
        P("clip", "tm", None),
        P("clip"),
        P("clip"),
        P(),
        P(),
        P(),
        P(),
    )
    return jax.shard_map(
        shards, mesh=mesh, in_specs=placed, out_specs=(P(), P(), P(), P(), P()), check_vma=False
    )
```

profile of v0, /device:TPU:2, one launch (start us, length us, event | category | flops | bytes accessed | tf_op | source)
XLA Modules:
  0.0 491.8 jit_solution(7356766110926714444)
XLA Ops:
  7.2 0.8 pad_maximum_fusion.5
  8.1 1.7 collective-permute-start
  9.8 1.3 collective-permute-start.1
  11.2 0.7 broadcast_compare_fusion
  12.0 1.3 compare_convert_fusion
  13.3 1.3 convert_reduce_fusion
  14.5 1.2 broadcast_compare_fusion.1
  15.8 104.9 %psum.43 = f32[]{:T(128)} all-reduce(f32[]{:T(128)} %convert_reduce_fusion), channel_id=1, replica_groups=mesh['clip'=32,'tm'=8] {'clip'}, use_global_device_ids=true, to_apply=%region_7.8 | all-reduce | flops 1 | bytes 8 | tf_op jit(solution)/shard_map/psum | solution.py:107
  121.4 1.5 pad_maximum_fusion.3
  123.7 1.0 fusion.30
  124.7 1.8 fusion.2
  127.1 1.0 fusion.29
  128.1 0.7 convolution_convert_fusion
  130.2 1.9 collective-permute-start.2
  132.1 1.3 collective-permute-start.3
  133.4 1.2 pad_maximum_fusion.1
  134.6 1.7 copy.1171
  136.3 2.6 copy.1167
  138.9 1.4 fusion
  142.9 2.3 fusion.28
  145.1 2.5 reshape.357
  147.7 1.5 pad.16
  149.2 2.6 reshape.358
  151.9 1.6 fusion.23
  153.5 2.8 multiply_reduce_fusion
  156.5 1.2 reshape.360
  157.9 1.7 reshape.361
  159.6 2.7 fusion.4
  162.3 1.7 convolution_bitcast_fusion
  164.1 2.2 fusion.20
  166.3 1.4 reshape.362
  167.8 1.1 slice.290
  168.9 3.1 reshape.363
  172.1 2.4 fusion.1
  174.5 6.2 %collective-permute-start.5 = (f32[4,15,512]{2,1,0:T(8,128)S(1)}, f32[4,15,512]{2,1,0:T(8,128)S(1)}, u32[]{:S(2)}, u32[]{:S(2)}) collective-permute-start(f32[4,15,512]{2,1,0:T(8,128)S(1)} %get-tuple-element.37), channel_id=1, source_target_pairs={{0,1},{1,2},{2,3},{3,4},{4,5},{5,6},{6,7},{8,9},{9,10},{10,11},{11... | collective-permute-start | bytes 368648 | tf_op jit(solution)/shard_map/ppermute | solution.py:32
  180.7 1.3 collective-permute-start.4
  182.0 2.2 fusion.36
  184.4 0.7 collective-permute-done.4
  186.3 1.4 copy-done.28
  187.7 1.7 convolution_bitcast_fusion.1
  189.5 1.2 fusion.19
  190.9 2.1 fusion.35
  194.3 90.7 %psum.42 = f32[]{:T(128)} all-reduce(f32[]{:T(128)} %select_reduce_fusion), channel_id=1, replica_groups=mesh['clip'=32,'tm'=8] {'clip','tm'}, use_global_device_ids=true, to_apply=%region_5.6 | all-reduce | flops 1 | bytes 8 | tf_op jit(solution)/shard_map/psum | solution.py:177
  286.3 190.9 %all-reduce.6.cloned.1.call-done = (f32[3,256,512]{2,1,0:T(8,128)}, f32[512,512]{1,0:T(8,128)}, f32[3,256,512]{2,1,0:T(8,128)}, f32[512,512]{1,0:T(8,128)}) async-done(((f32[3,256,512]{2,1,0:T(8,128)}, f32[512,512]{1,0:T(8,128)}, f32[3,256,512]{2,1,0:T(8,128)}, f32[512,512]{1,0:T(8,128)}), (f32[3,256,512]{2,1,0:T(8,128)}, f32[512,512]{1,0:T(8,128)}, f32[3,256,512]{2,1,0:T(8,128)}, ...) | async-done | bytes 5242896 | tf_op jit(solution)/shard_map/psum | solution.py:177
  477.3 2.8 copy.1216
  480.1 1.0 copy.1217
  481.1 1.1 copy.1218
  482.9 1.0 copy.1219
  (124 shorter events, 9.8 us)
Async XLA Ops:
  7.2 116.5 %copy-start = (bf16[3,256,512]{2,1,0:T(8,128)(2,1)S(1)}, bf16[3,256,512]{2,1,0:T(8,128)(2,1)}, u32[]{:S(2)}) copy-start(bf16[3,256,512]{2,1,0:T(8,128)(2,1)} %param.18) | copy-start | bytes 2359300
  7.2 470.1 %all-reduce.6.cloned.1.call-start = ((), (), s32[]{:S(2)}) async-start(), calls=%async_computation | async-start | bytes 10485760 | tf_op jit(solution)/shard_map/psum | solution.py:177
  8.1 113.3 %collective-permute-start = (bf16[2,4,1,256]{3,2,1,0:T(2,128)(2,1)S(1)}, bf16[2,4,1,256]{3,2,1,0:T(2,128)(2,1)S(1)}, u32[]{:S(2)}, u32[]{:S(2)}) collective-permute-start(bf16[2,4,1,256]{3,2,1,0:T(2,128)(2,1)S(1)} %get-tuple-element.45), channel_id=1, source_target_pairs={{0,1},{1,2},{2,3},{3,4},{4,5},{5,6},{6,7},{8,9},{9,10},{10,11},{11... | collective-permute-start | bytes 12296 | tf_op jit(solution)/shard_map/ppermute | solution.py:20
  9.8 111.5 %collective-permute-start.1 = (bf16[2,4,1,256]{3,2,1,0:T(2,128)(2,1)S(1)}, bf16[2,4,1,256]{3,2,1,0:T(2,128)(2,1)S(1)}, u32[]{:S(2)}, u32[]{:S(2)}) collective-permute-start(bf16[2,4,1,256]{3,2,1,0:T(2,128)(2,1)S(1)} %get-tuple-element.46), channel_id=1, source_target_pairs={{1,0},{2,1},{3,2},{4,3},{5,4},{6,5},{7,6},{9,8},{10,9},{11,10},{12... | collective-permute-start | bytes 12296 | tf_op jit(solution)/shard_map/ppermute | solution.py:22
  123.7 1.0 copy-start.22
  124.7 1.8 copy-start.29
  124.7 2.4 copy-start.21
  126.5 1.6 copy-start.13
  127.1 1.0 copy-start.24
  128.1 1.3 copy-start.27
  129.5 9.4 %copy-start.4 = (bf16[4,256,512]{2,1,0:T(8,128)(2,1)}, bf16[4,256,512]{2,1,0:T(8,128)(2,1)S(1)}, u32[]{:S(2)}) copy-start(bf16[4,256,512]{2,1,0:T(8,128)(2,1)S(1)} %convolution_convert_fusion) | copy-start | bytes 3145732
  130.2 8.7 %collective-permute-start.2 = (bf16[4,15,512]{2,1,0:T(8,128)(2,1)}, bf16[4,15,512]{2,1,0:T(8,128)(2,1)}, u32[]{:S(2)}, u32[]{:S(2)}) collective-permute-start(bf16[4,15,512]{2,1,0:T(8,128)(2,1)} %get-tuple-element.43), channel_id=1, source_target_pairs={{0,1},{1,2},{2,3},{3,4},{4,5},{5,6},{6,7},{8,9},{9,10},{10,11},{11... | collective-permute-start | bytes 184328 | tf_op jit(solution)/shard_map/ppermute | solution.py:20
  132.1 6.8 %collective-permute-start.3 = (bf16[4,15,512]{2,1,0:T(8,128)(2,1)}, bf16[4,15,512]{2,1,0:T(8,128)(2,1)}, u32[]{:S(2)}, u32[]{:S(2)}) collective-permute-start(bf16[4,15,512]{2,1,0:T(8,128)(2,1)} %get-tuple-element.44), channel_id=1, source_target_pairs={{1,0},{2,1},{3,2},{4,3},{5,4},{6,5},{7,6},{9,8},{10,9},{11,10},{12... | collective-permute-start | bytes 184328 | tf_op jit(solution)/shard_map/ppermute | solution.py:22
  147.7 4.2 copy-start.9
  147.7 4.2 copy-start.11
  147.7 4.2 copy-start.15
  147.7 4.2 copy-start.17
  149.2 4.3 copy-start.19
  149.2 4.3 copy-start.10
  149.2 4.3 copy-start.18
  151.9 4.5 copy-start.14
  159.6 2.7 copy-start.8
  159.6 2.7 copy-start.30
  162.3 1.8 copy-start.23
  168.9 3.2 copy-start.5
  172.1 9.9 %copy-start.2 = (bf16[768,1024]{1,0:T(8,128)(2,1)S(1)}, bf16[768,1024]{1,0:T(8,128)(2,1)}, u32[]{:S(2)}) copy-start(bf16[768,1024]{1,0:T(8,128)(2,1)} %copy.1171) | copy-start | bytes 4718596
  172.1 9.9 %copy-start.26 = (bf16[1024,512,1]{1,0,2:T(8,128)(2,1)S(1)}, bf16[1024,512,1]{1,0,2:T(8,128)(2,1)}, u32[]{:S(2)}) copy-start(bf16[1024,512,1]{1,0,2:T(8,128)(2,1)} %fusion.20) | copy-start | bytes 3145732
  174.5 11.2 %collective-permute-start.5 = (f32[4,15,512]{2,1,0:T(8,128)S(1)}, f32[4,15,512]{2,1,0:T(8,128)S(1)}, u32[]{:S(2)}, u32[]{:S(2)}) collective-permute-start(f32[4,15,512]{2,1,0:T(8,128)S(1)} %get-tuple-element.37), channel_id=1, source_target_pairs={{0,1},{1,2},{2,3},{3,4},{4,5},{5,6},{6,7},{8,9},{9,10},{10,11},{11... | collective-permute-start | bytes 368648 | tf_op jit(solution)/shard_map/ppermute | solution.py:32
  180.7 4.5 collective-permute-start.4
  186.1 1.6 copy-start.28
  187.7 1.8 copy-start.25
  189.5 1.4 copy-start.1
  193.0 0.7 copy-start.12
  193.0 0.7 copy-start.16
  193.0 0.7 copy-start.20
  477.3 2.8 copy-start.7
  477.3 3.8 copy-start.3
  481.1 1.8 copy-start.6
Sparse Core Ops, SparseCore 0:
  193.1 284.1 all-reduce.5
where the time goes:
time: 493 us; the launch traced here: 492 us
  blocking collectives  196 us (40%)
  waiting for transfers between devices  192 us (39%)
  local copies, waits for them, and re-layouts  34.6 us (7%)
  matrix products  22.9 us (5%)
  between operations  17.7 us (4%)
  other arithmetic  15.7 us (3%)
  starting transfers between devices  13.7 us (3%)
    psum x1, waiting for transfers between devices, shards(): lax.psum((grad_ac, grad_vc, grad_ap, grad_vp, loss_local), ('clip', 'tm'))  191 us
    psum x1, blocking collectives, shards(): lax.psum(jnp.sum((lengths - jnp.abs(labels)).astype(jnp.float32)), 'clip')  105 us
    psum x1, blocking collectives, shards(): lax.psum((grad_ac, grad_vc, grad_ap, grad_vp, loss_local), ('clip', 'tm'))  90.7 us
    unnamed x96, local copies, waits for them, and re-layouts  12 us
  transfers between devices with their start and end apart: 7, of which 2 were waited for; matrix products, arithmetic and copies ran while one was open for 3% of the time, Pallas kernels for 0%

commit v1 on v0

--- a/solution.py
+++ b/solution.py
@@ -174,8 +174,8 @@
     grad_vp = proj_grad(hid_v, grad_lip)
     grad_ac = conv_grad(cols_a, pre_a, grad_audio, w_audio_proj, w_audio_conv)
     grad_vc = conv_grad(cols_v, pre_v, grad_lip, w_lip_proj, w_lip_conv)
-    grad_ac, grad_vc, grad_ap, grad_vp, loss_sum = lax.psum(
-        (grad_ac, grad_vc, grad_ap, grad_vp, loss_local), ("clip", "tm")
+    grad_ac, grad_vc, grad_ap, grad_vp, loss_sum = jax.lax.psum(
+        jax.lax.psum((grad_ac, grad_vc, grad_ap, grad_vp, loss_local), "clip"), axis_name="tm"
     )
     return (loss_sum / count, grad_ac, grad_ap, grad_vc, grad_vp)
 

time: 493 us -> 840 us (1.70)
  waiting for transfers between devices: 192 us -> 506 us
  blocking collectives: 196 us -> 234 us
    psum x1 -> x2, waiting for transfers between devices: 191 us -> 505 us  [the longest x1 490 us: shards(): jax.lax.psum((grad_ac, grad_vc, grad_ap, grad_vp, loss_local), 'clip')]
    psum x1 -> x2, blocking collectives: 90.7 us -> 129 us  [the longest x1 114 us: shards(): jax.lax.psum((grad_ac, grad_vc, grad_ap, grad_vp, loss_local), 'clip')]
  transfers between devices with their start and end apart: 7 -> 8, of which waited for: 2 -> 3; matrix products, arithmetic and copies ran while one was open for 3% -> 2% of each run, Pallas kernels for 0% -> 0%
where the time goes in v1:
time: 840 us; the launch traced here: 838 us
  waiting for transfers between devices  506 us (60%)
  blocking collectives  234 us (28%)
  local copies, waits for them, and re-layouts  30.6 us (4%)
  matrix products  22 us (3%)
  between operations  17.9 us (2%)
  other arithmetic  14.6 us (2%)
  starting transfers between devices  13.8 us (2%)
    psum x1, waiting for transfers between devices, shards(): jax.lax.psum((grad_ac, grad_vc, grad_ap, grad_vp, loss_local), 'clip')  490 us
    psum x1, blocking collectives, shards(): jax.lax.psum((grad_ac, grad_vc, grad_ap, grad_vp, loss_local), 'clip')  114 us
    psum x1, blocking collectives, shards(): lax.psum(jnp.sum((lengths - jnp.abs(labels)).astype(jnp.float32)), 'clip')  105 us
  transfers between devices with their start and end apart: 8, of which 3 were waited for; matrix products, arithmetic and copies ran while one was open for 2% of the time, Pallas kernels for 0%

profile of v1, /device:TPU:2, one launch (start us, length us, event | category | flops | bytes accessed | tf_op | source)
XLA Modules:
  0.0 838.1 jit_solution(9309386993413096230)
XLA Ops:
  7.2 0.8 pad_maximum_fusion.5
  8.1 1.7 collective-permute-start
  9.8 1.3 collective-permute-start.1
  11.2 0.7 broadcast_compare_fusion
  11.9 0.8 broadcast_add_fusion
  12.6 1.3 compare_convert_fusion
  13.9 1.3 convert_reduce_fusion
  15.2 1.3 broadcast_compare_fusion.1
  16.5 104.9 %psum.79 = f32[]{:T(128)} all-reduce(f32[]{:T(128)} %convert_reduce_fusion), channel_id=1, replica_groups=mesh['clip'=32,'tm'=8] {'clip'}, use_global_device_ids=true, to_apply=%region_8.9 | all-reduce | flops 1 | bytes 8 | tf_op jit(solution)/shard_map/psum | solution.py:107
  122.1 1.5 pad_maximum_fusion.3
  124.4 1.0 fusion.30
  125.4 1.8 fusion.2
  127.2 1.0 fusion.29
  128.3 0.7 convolution_convert_fusion
  129.6 1.3 collective-permute-start.2
  130.9 1.3 collective-permute-start.3
  132.2 1.2 pad_maximum_fusion.1
  133.5 1.6 copy.1171
  135.1 2.7 copy.1167
  141.0 1.9 fusion.28
  142.9 1.6 reshape.357
  144.8 1.5 reshape.358
  146.9 2.2 multiply_reduce_fusion
  149.3 1.2 reshape.360
  150.7 1.7 reshape.361
  152.4 2.3 fusion.4
  154.8 1.8 convolution_bitcast_fusion
  156.5 2.2 fusion.20
  158.8 1.4 reshape.362
  160.3 1.1 slice.290
  161.4 3.1 reshape.363
  165.2 0.7 fusion.24
  166.0 2.1 fusion.1
  168.1 6.8 collective-permute-start.5
  174.9 1.3 collective-permute-start.4
  176.2 2.2 fusion.36
  180.5 1.4 copy-done.38
  181.9 1.8 convolution_bitcast_fusion.1
  183.7 1.2 fusion.19
  185.1 2.1 fusion.35
  187.3 489.6 %all-reduce.8.cloned.1.call-done = (f32[3,256,512]{2,1,0:T(8,128)}, f32[512,512]{1,0:T(8,128)}, f32[3,256,512]{2,1,0:T(8,128)}, f32[512,512]{1,0:T(8,128)}) async-done(((f32[3,256,512]{2,1,0:T(8,128)}, f32[512,512]{1,0:T(8,128)}, f32[3,256,512]{2,1,0:T(8,128)}, f32[512,512]{1,0:T(8,128)}), (f32[3,256,512]{2,1,0:T(8,128)}, f32[512,512]{1,0:T(8,128)}, f32[3,256,512]{2,1,0:T(8,128)}, ...) | async-done | bytes 5242896 | tf_op jit(solution)/shard_map/psum | solution.py:178
  678.2 114.3 %psum.77 = f32[]{:T(128)} all-reduce(f32[]{:T(128)} %select_reduce_fusion), channel_id=1, replica_groups=mesh['clip'=32,'tm'=8] {'clip'}, use_global_device_ids=true, to_apply=%region_5.6 | all-reduce | flops 1 | bytes 8 | tf_op jit(solution)/shard_map/psum | solution.py:178
  792.5 14.5 %psum.78 = f32[]{:T(128)} all-reduce(f32[]{:T(128)} %psum.77), channel_id=1, replica_groups=mesh['clip'=32,'tm'=8] {'tm'}, use_global_device_ids=true, to_apply=%region_6.7 | all-reduce | flops 1 | bytes 8 | tf_op jit(solution)/shard_map/psum | solution.py:177
  808.3 15.2 %all-reduce.10.cloned.1.call-done = (f32[3,256,512]{2,1,0:T(8,128)}, f32[512,512]{1,0:T(8,128)}, f32[3,256,512]{2,1,0:T(8,128)}, f32[512,512]{1,0:T(8,128)}) async-done(((f32[3,256,512]{2,1,0:T(8,128)}, f32[512,512]{1,0:T(8,128)}, f32[3,256,512]{2,1,0:T(8,128)}, f32[512,512]{1,0:T(8,128)}), (f32[3,256,512]{2,1,0:T(8,128)}, f32[512,512]{1,0:T(8,128)}, f32[3,256,512]{2,1,0:T(8,128)}, ...) | async-done | bytes 5242896 | tf_op jit(solution)/shard_map/psum | solution.py:177
  823.5 2.8 copy.1220
  826.4 1.0 copy.1221
  827.3 1.1 copy.1222
  829.1 1.0 copy.1223
  (148 shorter events, 11.1 us)
Async XLA Ops:
  7.2 117.2 %copy-start = (bf16[3,256,512]{2,1,0:T(8,128)(2,1)S(1)}, bf16[3,256,512]{2,1,0:T(8,128)(2,1)}, u32[]{:S(2)}) copy-start(bf16[3,256,512]{2,1,0:T(8,128)(2,1)} %param.18) | copy-start | bytes 2359300
  7.2 669.6 %all-reduce.8.cloned.1.call-start = ((), (), s32[]{:S(2)}) async-start(), calls=%async_computation | async-start | bytes 10485760 | tf_op jit(solution)/shard_map/psum | solution.py:178
  8.1 114.0 %collective-permute-start = (bf16[2,4,1,256]{3,2,1,0:T(2,128)(2,1)S(1)}, bf16[2,4,1,256]{3,2,1,0:T(2,128)(2,1)S(1)}, u32[]{:S(2)}, u32[]{:S(2)}) collective-permute-start(bf16[2,4,1,256]{3,2,1,0:T(2,128)(2,1)S(1)} %get-tuple-element.49), channel_id=1, source_target_pairs={{0,1},{1,2},{2,3},{3,4},{4,5},{5,6},{6,7},{8,9},{9,10},{10,11},{11... | collective-permute-start | bytes 12296 | tf_op jit(solution)/shard_map/ppermute | solution.py:20
  9.8 112.3 %collective-permute-start.1 = (bf16[2,4,1,256]{3,2,1,0:T(2,128)(2,1)S(1)}, bf16[2,4,1,256]{3,2,1,0:T(2,128)(2,1)S(1)}, u32[]{:S(2)}, u32[]{:S(2)}) collective-permute-start(bf16[2,4,1,256]{3,2,1,0:T(2,128)(2,1)S(1)} %get-tuple-element.50), channel_id=1, source_target_pairs={{1,0},{2,1},{3,2},{4,3},{5,4},{6,5},{7,6},{9,8},{10,9},{11,10},{12... | collective-permute-start | bytes 12296 | tf_op jit(solution)/shard_map/ppermute | solution.py:22
  124.4 1.0 copy-start.31
  125.4 1.8 copy-start.39
  125.4 1.8 copy-start.30
  127.2 1.0 copy-start.22
  127.2 1.0 copy-start.33
  128.3 1.3 copy-start.37
  129.6 11.4 %copy-start.6 = (bf16[4,256,512]{2,1,0:T(8,128)(2,1)}, bf16[4,256,512]{2,1,0:T(8,128)(2,1)S(1)}, u32[]{:S(2)}) copy-start(bf16[4,256,512]{2,1,0:T(8,128)(2,1)S(1)} %convolution_convert_fusion) | copy-start | bytes 3145732
  129.6 8.2 collective-permute-start.2
  130.9 6.9 collective-permute-start.3
  135.1 5.9 copy-start.35
  137.8 5.2 copy-start.15
  137.8 5.1 copy-start.18
  144.5 1.8 copy-start.9
  144.5 1.8 copy-start.14
  144.5 1.8 copy-start.24
  144.5 1.8 copy-start.26
  144.8 2.1 copy-start.28
  144.8 2.2 copy-start.27
  146.3 2.8 copy-start.23
  149.3 3.1 copy-start.7
  149.3 3.1 copy-start.16
  149.3 3.1 copy-start.19
  152.4 2.3 copy-start.12
  152.4 2.3 copy-start.40
  154.8 1.8 copy-start.32
  156.5 2.2 copy-start.2
  161.4 4.6 copy-start.8
  161.4 4.6 copy-start.13
  161.4 4.6 copy-start.17
  161.4 4.6 copy-start.20
  165.9 10.3 %copy-start.4 = (bf16[768,1024]{1,0:T(8,128)(2,1)S(1)}, bf16[768,1024]{1,0:T(8,128)(2,1)}, u32[]{:S(2)}) copy-start(bf16[768,1024]{1,0:T(8,128)(2,1)} %copy.1171) | copy-start | bytes 4718596
  165.9 10.3 %copy-start.36 = (bf16[1024,512,1]{1,0,2:T(8,128)(2,1)S(1)}, bf16[1024,512,1]{1,0,2:T(8,128)(2,1)}, u32[]{:S(2)}) copy-start(bf16[1024,512,1]{1,0,2:T(8,128)(2,1)} %fusion.20) | copy-start | bytes 3145732
  168.1 11.8 %collective-permute-start.5 = (f32[4,15,512]{2,1,0:T(8,128)S(1)}, f32[4,15,512]{2,1,0:T(8,128)S(1)}, u32[]{:S(2)}, u32[]{:S(2)}) collective-permute-start(f32[4,15,512]{2,1,0:T(8,128)S(1)} %get-tuple-element.41), channel_id=1, source_target_pairs={{0,1},{1,2},{2,3},{3,4},{4,5},{5,6},{6,7},{8,9},{9,10},{10,11},{11... | collective-permute-start | bytes 368648 | tf_op jit(solution)/shard_map/ppermute | solution.py:32
  174.9 4.5 collective-permute-start.4
  180.3 1.6 copy-start.38
  181.9 1.8 copy-start.34
  183.7 1.4 copy-start.3
  187.2 636.3 %all-reduce.10.cloned.1.call-start = ((), (), s32[]{:S(2)}) async-start(), calls=%async_computation.1 | async-start | bytes 10485760 | tf_op jit(solution)/shard_map/psum | solution.py:177
  676.8 0.7 copy-start.25
  676.8 0.7 copy-start.29
  823.5 2.8 copy-start.11
  823.5 3.8 copy-start.5
  826.4 3.7 copy-start.1
  827.3 1.8 copy-start.10
  (1 other events, 0.7 us)
Sparse Core Ops, SparseCore 0:
  187.3 489.4 all-reduce.7
  679.7 143.7 all-reduce.9
